TPU v7x, 512 devices: a whole 4x8x8 slice. The times are simulated.
512 devices in a mesh: depth: 8 (over z_hi, x), gx: 8 (over y), gy: 8 (over z_lo, core).
Axes of the slice: x: 4, y: 8, z: 8 (z_hi: 2, z_lo: 4; z = z_hi * 4 + z_lo), core: 2. Of those that a mesh axis runs over, the one named last changes fastest.
Arguments:
- arrival: bfloat16 [8, 192, 8, 8, 896], P('depth', None, 'gx', 'gy'), may hold values from -6 to 6
- source: bfloat16 [8, 4, 192, 8, 8, 896], P('depth', None, None, 'gx', 'gy'), may hold values from -6 to 6
- assignment: int32 [4, 192], replicated, may hold values from 0 to 191, each once within a row
- counts: int32 [11, 12, 8, 8], P(None, None, 'gx', 'gy'), may hold values from 1 to 16
- first_map: bfloat16 [8, 8, 8, 896, 896], P('depth', 'gx', 'gy'), may hold values from -0.1875 to 0.1875
- second_map: bfloat16 [8, 8, 8, 896, 896], P('depth', 'gx', 'gy'), may hold values from -0.1875 to 0.1875
- damping: float32 [8, 8, 8, 896], P('depth', 'gx', 'gy'), may hold values from 0.2 to 0.9
Outputs:
- final_traces: bfloat16 [8, 192, 8, 8, 896], P('depth', None, 'gx', 'gy')
Inputs may be any that keep to these rules, and one draw needn't show every extreme that they name: Each row of assignment is a permutation of the 192 shots.
All inputs are finite; a program needn't handle non-finite values.
Results may differ from a plain program's by a relative error of at most 0.017.
Values may be sent and summed in bfloat16 or wider, within the bound.
A program may use at most 64 MiB of HBM per device.

v0:
```python
import jax
import jax.numpy as jnp
from jax import lax
from jax.sharding import PartitionSpec as P

FX = 32
FY = 28
SHOT_BATCH = 16


coupling_weight = 0.25


def with_halo(x, sides, width):
    edges = {}
    for axis, dim in sides:
        count, length = (lax.axis_size(axis), x.shape[dim])
        up = [(i, (i + 1) % count) for i in range(count - 1)]
        last = lax.slice_in_dim(x, length - width, length, axis=dim)
        first = lax.slice_in_dim(x, 0, width, axis=dim)
        edges[dim] = (
            lax.ppermute(last, axis, up),
            lax.ppermute(first, axis, [(b, a) for a, b in up]),
        )
    done = []
    for _, dim in sides:
        low, high = edges[dim]
        around = [(width, width) if d in done else (0, 0) for d in range(x.ndim)]
        x = jnp.concatenate([jnp.pad(low, around), x, jnp.pad(high, around)], axis=dim)
        done.append(dim)
    return x


def shifted(x, axis, by):
    count = lax.axis_size(axis)
    pairs = [(i, i + by) for i in range(count) if 0 <= i + by < count]
    return lax.ppermute(x, axis, pairs)


def neighbour_sum(padded):
    widened = padded.astype(jnp.float32)
    return (
        widened[:, 2:, 1:-1] + widened[:, :-2, 1:-1] + widened[:, 1:-1, 2:] + widened[:, 1:-1, :-2]
    )


def advance(incoming, picked, active, map_first, map_second, damping_now, swap_faces):
    slot_count = incoming.shape[0]
    start_trace = (active * (picked.astype(jnp.float32) + incoming.astype(jnp.float32))).astype(
        jnp.bfloat16
    )
    mapped = jnp.dot(start_trace, map_first, preferred_element_type=jnp.float32).astype(
        jnp.bfloat16
    )
    face_grid = mapped.reshape(slot_count, FX, FY)
    padded = swap_faces(face_grid)
    coupled = (face_grid.astype(jnp.float32) + coupling_weight * neighbour_sum(padded)).astype(
        jnp.bfloat16
    )
    imaged = jnp.dot(
        coupled.reshape(slot_count, FX * FY), map_second, preferred_element_type=jnp.float32
    )
    blended = damping_now * imaged + (1.0 - damping_now) * start_trace.astype(jnp.float32)
    return (active * blended).astype(jnp.bfloat16)


def local(arrival, source, assignment, counts, first_map, second_map, damping):
    map_first = first_map[0, 0, 0]
    map_second = second_map[0, 0, 0]
    damping_now = damping[0, 0, 0][None, :]
    layer_index = lax.axis_index("depth")
    section_count = lax.axis_size("depth")
    slot_count = arrival.shape[1]
    round_count = source.shape[1]
    positions = jnp.arange(SHOT_BATCH, dtype=jnp.int32)
    live_table = counts[:, :, 0, 0]
    incoming = arrival[0, :, 0, 0, :]

    def faces_whole(face_grid):
        return with_halo(face_grid, (("gx", 1), ("gy", 2)), 1)

    for round_number in range(round_count):
        unit_index = round_number - layer_index + section_count - 1
        live_counts = lax.dynamic_index_in_dim(live_table, unit_index, 0, keepdims=False)
        active = (
            (positions[None, :] < live_counts[:, None]).reshape(slot_count, 1).astype(jnp.float32)
        )
        picked = jnp.take(source[0, round_number, :, 0, 0, :], assignment[round_number], axis=0)
        final_round = round_number == round_count - 1
        traces = advance(incoming, picked, active, map_first, map_second, damping_now, faces_whole)
        if not final_round:
            traces = shifted(traces, "depth", 1)
        incoming = traces
    return incoming.reshape(1, slot_count, 1, 1, incoming.shape[1])


def solution(mesh):
    return jax.shard_map(
        local,
        mesh=mesh,
        in_specs=(
            P("depth", None, "gx", "gy", None),
            P("depth", None, None, "gx", "gy", None),
            P(),
            P(None, None, "gx", "gy"),
            P("depth", "gx", "gy", None, None),
            P("depth", "gx", "gy", None, None),
            P("depth", "gx", "gy", None),
        ),
        out_specs=P("depth", None, "gx", "gy", None),
        check_vma=False,
    )
```

profile of v0, /device:TPU:328, one launch (start us, length us, event | category | flops | bytes accessed | tf_op | source)
XLA Modules:
  0.0 158.3 jit_solution(150421581581009184)
XLA Ops:
  12.4 3.6 %collective-permute-start.3 = (bf16[192,32,1]{0,2,1:T(2,128)(2,1)}, bf16[192,32,1]{0,2,1:T(2,128)(2,1)}, u32[]{:S(2)}, u32[]{:S(2)}) collective-permute-start(bf16[192,32,1]{0,2,1:T(2,128)(2,1)} %get-tuple-element.25), channel_id=1, source_target_pairs={{1,0},{2,1},{3,2},{4,3},{5,4},{6,5},{7,6},{9,8},{10,9},{11,10},{12... | collective-permute-start | bytes 36872 | tf_op jit(solution)/shard_map/ppermute | solution.py:23
  16.6 3.5 %collective-permute-start.1 = (bf16[192,1,28]{0,2,1:T(8,128)(2,1)}, bf16[192,1,28]{0,2,1:T(8,128)(2,1)S(1)}, u32[]{:S(2)}, u32[]{:S(2)}) collective-permute-start(bf16[192,1,28]{0,2,1:T(8,128)(2,1)} %get-tuple-element.22), channel_id=1, source_target_pairs={{0,8},{8,16},{16,24},{24,32},{32,40},{40,48},{48,56},{1,9},{9,17},... | collective-permute-start | bytes 32264 | tf_op jit(solution)/shard_map/ppermute | solution.py:22
  20.1 2.4 %collective-permute-start.2 = (bf16[192,1,28]{0,2,1:T(8,128)(2,1)}, bf16[192,1,28]{0,2,1:T(8,128)(2,1)}, u32[]{:S(2)}, u32[]{:S(2)}) collective-permute-start(bf16[192,1,28]{0,2,1:T(8,128)(2,1)} %get-tuple-element.23), channel_id=1, source_target_pairs={{8,0},{16,8},{24,16},{32,24},{40,32},{48,40},{56,48},{9,1},{17,9},... | collective-permute-start | bytes 32264 | tf_op jit(solution)/shard_map/ppermute | solution.py:23
  29.6 2.9 %fusion.52 = bf16[192,896]{1,0:T(8,128)(2,1)} fusion(bf16[192,896]{0,1:T(8,128)(2,1)S(1)} %reshape.131, bf16[1,1,1,896,896]{4,3,2,1,0:T(8,128)(2,1)} %param.14, f32[896]{0:T(1024)S(1)} %copy-done.3, f32[192]{0:T(256)S(1)} %copy-done.13, f32[896]{0:T(1024)S(1)} %copy-done.2, bf16[1,192,1,1,896]{4,1,3,2,0:T(8,128)(2,1)} %param.9, ...), kind=kOutput, calls=%fused_computation.32 | convolution fusion | flops 310345728 | bytes 2990016 | tf_op jit(solution)/shard_map/dot_general | solution.py:60
  32.5 3.4 %collective-permute-start.4 = (bf16[192,896]{1,0:T(8,128)(2,1)}, bf16[192,896]{1,0:T(8,128)(2,1)}, u32[]{:S(2)}, u32[]{:S(2)}) collective-permute-start(bf16[192,896]{1,0:T(8,128)(2,1)} %fusion.52), channel_id=1, source_target_pairs={{0,64},{64,128},{128,192},{192,256},{256,320},{320,384},{384,448},... | collective-permute-start | bytes 1032200 | tf_op jit(solution)/shard_map/ppermute | solution.py:37
  37.2 19.4 %collective-permute-done.4 = bf16[192,896]{1,0:T(8,128)(2,1)} collective-permute-done((bf16[192,896]{1,0:T(8,128)(2,1)}, bf16[192,896]{1,0:T(8,128)(2,1)}, u32[]{:S(2)}, u32[]{:S(2)}) %collective-permute-start.4) | collective-permute-done | bytes 344096 | tf_op jit(solution)/shard_map/ppermute | solution.py:37
  60.5 3.6 %collective-permute-start.8 = (bf16[192,32,1]{0,2,1:T(2,128)(2,1)S(1)}, bf16[192,32,1]{0,2,1:T(2,128)(2,1)S(1)}, u32[]{:S(2)}, u32[]{:S(2)}) collective-permute-start(bf16[192,32,1]{0,2,1:T(2,128)(2,1)S(1)} %get-tuple-element.21), channel_id=1, source_target_pairs={{1,0},{2,1},{3,2},{4,3},{5,4},{6,5},{7,6},{9,8},{10,9},{11,10},{12... | collective-permute-start | bytes 36872 | tf_op jit(solution)/shard_map/ppermute | solution.py:23
  64.1 4.5 %collective-permute-start.6 = (bf16[192,1,28]{0,2,1:T(8,128)(2,1)S(1)}, bf16[192,1,28]{0,2,1:T(8,128)(2,1)S(1)}, u32[]{:S(2)}, u32[]{:S(2)}) collective-permute-start(bf16[192,1,28]{0,2,1:T(8,128)(2,1)S(1)} %get-tuple-element.18), channel_id=1, source_target_pairs={{0,8},{8,16},{16,24},{24,32},{32,40},{40,48},{48,56},{1,9},{9,17},... | collective-permute-start | bytes 32264 | tf_op jit(solution)/shard_map/ppermute | solution.py:22
  70.7 4.5 %collective-permute-done.7 = bf16[192,1,28]{0,2,1:T(8,128)(2,1)S(1)} collective-permute-done((bf16[192,1,28]{0,2,1:T(8,128)(2,1)S(1)}, bf16[192,1,28]{0,2,1:T(8,128)(2,1)S(1)}, u32[]{:S(2)}, u32[]{:S(2)}) %collective-permute-start.7) | collective-permute-done | bytes 10784 | tf_op jit(solution)/shard_map/ppermute | solution.py:23
  76.2 3.0 %fusion.55 = bf16[192,896]{1,0:T(8,128)(2,1)} fusion(bf16[192,896]{0,1:T(8,128)(2,1)S(1)} %reshape.133, bf16[1,1,1,896,896]{4,3,2,1,0:T(8,128)(2,1)} %param.14, f32[896]{0:T(1024)S(1)} %copy-done.3, f32[192]{0:T(256)S(1)} %reshape.141, f32[896]{0:T(1024)S(1)} %copy-done.2, bf16[192,896]{1,0:T(8,128)(2,1)} %collective-permute-done.4, ...), kind=kOutput, calls=%fused_computation.33 | convolution fusion | flops 310345728 | bytes 2990016 | tf_op jit(solution)/shard_map/dot_general | solution.py:60
  82.2 17.4 %collective-permute-done.9 = bf16[192,896]{1,0:T(8,128)(2,1)S(1)} collective-permute-done((bf16[192,896]{1,0:T(8,128)(2,1)}, bf16[192,896]{1,0:T(8,128)(2,1)S(1)}, u32[]{:S(2)}, u32[]{:S(2)}) %collective-permute-start.9) | collective-permute-done | bytes 344096 | tf_op jit(solution)/shard_map/ppermute | solution.py:37
  101.4 1.9 %collective-permute-start.10 = (bf16[192,32,1]{0,2,1:T(2,128)(2,1)S(1)}, bf16[192,32,1]{0,2,1:T(2,128)(2,1)S(1)}, u32[]{:S(2)}, u32[]{:S(2)}) collective-permute-start(bf16[192,32,1]{0,2,1:T(2,128)(2,1)S(1)} %get-tuple-element.16), channel_id=1, source_target_pairs={{0,1},{1,2},{2,3},{3,4},{4,5},{5,6},{6,7},{8,9},{9,10},{10,11},{11... | collective-permute-start | bytes 36872 | tf_op jit(solution)/shard_map/ppermute | solution.py:22
  103.4 3.6 %collective-permute-start.13 = (bf16[192,32,1]{0,2,1:T(2,128)(2,1)S(1)}, bf16[192,32,1]{0,2,1:T(2,128)(2,1)S(1)}, u32[]{:S(2)}, u32[]{:S(2)}) collective-permute-start(bf16[192,32,1]{0,2,1:T(2,128)(2,1)S(1)} %get-tuple-element.17), channel_id=1, source_target_pairs={{1,0},{2,1},{3,2},{4,3},{5,4},{6,5},{7,6},{9,8},{10,9},{11,10},{12... | collective-permute-start | bytes 36872 | tf_op jit(solution)/shard_map/ppermute | solution.py:23
  107.0 3.6 %collective-permute-start.11 = (bf16[192,1,28]{0,2,1:T(8,128)(2,1)S(1)}, bf16[192,1,28]{0,2,1:T(8,128)(2,1)S(1)}, u32[]{:S(2)}, u32[]{:S(2)}) collective-permute-start(bf16[192,1,28]{0,2,1:T(8,128)(2,1)S(1)} %get-tuple-element.14), channel_id=1, source_target_pairs={{0,8},{8,16},{16,24},{24,32},{32,40},{40,48},{48,56},{1,9},{9,17},... | collective-permute-start | bytes 32264 | tf_op jit(solution)/shard_map/ppermute | solution.py:22
  110.7 2.2 %collective-permute-start.12 = (bf16[192,1,28]{0,2,1:T(8,128)(2,1)S(1)}, bf16[192,1,28]{0,2,1:T(8,128)(2,1)S(1)}, u32[]{:S(2)}, u32[]{:S(2)}) collective-permute-start(bf16[192,1,28]{0,2,1:T(8,128)(2,1)S(1)} %get-tuple-element.15), channel_id=1, source_target_pairs={{8,0},{16,8},{24,16},{32,24},{40,32},{48,40},{56,48},{9,1},{17,9},... | collective-permute-start | bytes 32264 | tf_op jit(solution)/shard_map/ppermute | solution.py:23
  112.9 3.4 %collective-permute-done.12 = bf16[192,1,28]{0,2,1:T(8,128)(2,1)S(1)} collective-permute-done((bf16[192,1,28]{0,2,1:T(8,128)(2,1)S(1)}, bf16[192,1,28]{0,2,1:T(8,128)(2,1)S(1)}, u32[]{:S(2)}, u32[]{:S(2)}) %collective-permute-start.12) | collective-permute-done | bytes 10784 | tf_op jit(solution)/shard_map/ppermute | solution.py:23
  117.2 2.1 %fusion.58 = bf16[192,896]{1,0:T(8,128)(2,1)S(1)} fusion(bf16[192,896]{0,1:T(8,128)(2,1)S(1)} %reshape.135, bf16[1,1,1,896,896]{4,3,2,1,0:T(8,128)(2,1)} %param.14, f32[896]{0:T(1024)S(1)} %copy-done.3, f32[192]{0:T(256)S(1)} %reshape.140, f32[896]{0:T(1024)S(1)} %copy-done.2, bf16[192,896]{1,0:T(8,128)(2,1)} %copy-done.16, ...), kind=kOutput, calls=%fused_computation.34 | convolution fusion | flops 310345728 | bytes 2990016 | tf_op jit(solution)/shard_map/dot_general | solution.py:60
  119.3 2.1 %collective-permute-start.14 = (bf16[192,896]{1,0:T(8,128)(2,1)S(1)}, bf16[192,896]{1,0:T(8,128)(2,1)S(1)}, u32[]{:S(2)}, u32[]{:S(2)}) collective-permute-start(bf16[192,896]{1,0:T(8,128)(2,1)S(1)} %fusion.58), channel_id=1, source_target_pairs={{0,64},{64,128},{128,192},{192,256},{256,320},{320,384},{384,448},... | collective-permute-start | bytes 1032200 | tf_op jit(solution)/shard_map/ppermute | solution.py:37
  122.7 15.6 %collective-permute-done.14 = bf16[192,896]{1,0:T(8,128)(2,1)S(1)} collective-permute-done((bf16[192,896]{1,0:T(8,128)(2,1)S(1)}, bf16[192,896]{1,0:T(8,128)(2,1)S(1)}, u32[]{:S(2)}, u32[]{:S(2)}) %collective-permute-start.14) | collective-permute-done | bytes 344096 | tf_op jit(solution)/shard_map/ppermute | solution.py:37
  141.3 3.6 %collective-permute-start.18 = (bf16[192,32,1]{0,2,1:T(2,128)(2,1)S(1)}, bf16[192,32,1]{0,2,1:T(2,128)(2,1)S(1)}, u32[]{:S(2)}, u32[]{:S(2)}) collective-permute-start(bf16[192,32,1]{0,2,1:T(2,128)(2,1)S(1)} %get-tuple-element.13), channel_id=1, source_target_pairs={{1,0},{2,1},{3,2},{4,3},{5,4},{6,5},{7,6},{9,8},{10,9},{11,10},{12... | collective-permute-start | bytes 36872 | tf_op jit(solution)/shard_map/ppermute | solution.py:23
  145.0 3.6 %collective-permute-start.16 = (bf16[192,1,28]{0,2,1:T(8,128)(2,1)S(1)}, bf16[192,1,28]{0,2,1:T(8,128)(2,1)S(1)}, u32[]{:S(2)}, u32[]{:S(2)}) collective-permute-start(bf16[192,1,28]{0,2,1:T(8,128)(2,1)S(1)} %get-tuple-element.10), channel_id=1, source_target_pairs={{0,8},{8,16},{16,24},{24,32},{32,40},{40,48},{48,56},{1,9},{9,17},... | collective-permute-start | bytes 32264 | tf_op jit(solution)/shard_map/ppermute | solution.py:22
  148.6 2.2 %collective-permute-start.17 = (bf16[192,1,28]{0,2,1:T(8,128)(2,1)S(1)}, bf16[192,1,28]{0,2,1:T(8,128)(2,1)S(1)}, u32[]{:S(2)}, u32[]{:S(2)}) collective-permute-start(bf16[192,1,28]{0,2,1:T(8,128)(2,1)S(1)} %get-tuple-element.11), channel_id=1, source_target_pairs={{8,0},{16,8},{24,16},{32,24},{40,32},{48,40},{56,48},{9,1},{17,9},... | collective-permute-start | bytes 32264 | tf_op jit(solution)/shard_map/ppermute | solution.py:23
  150.8 3.4 %collective-permute-done.17 = bf16[192,1,28]{0,2,1:T(8,128)(2,1)S(1)} collective-permute-done((bf16[192,1,28]{0,2,1:T(8,128)(2,1)S(1)}, bf16[192,1,28]{0,2,1:T(8,128)(2,1)S(1)}, u32[]{:S(2)}, u32[]{:S(2)}) %collective-permute-start.17) | collective-permute-done | bytes 10784 | tf_op jit(solution)/shard_map/ppermute | solution.py:23
  155.5 2.8 %fusion.76 = bf16[1,192,1,1,896]{4,1,3,2,0:T(8,128)(2,1)} fusion(bf16[192,896]{0,1:T(8,128)(2,1)S(1)} %reshape.137, bf16[1,1,1,896,896]{4,3,2,1,0:T(8,128)(2,1)} %param.14, f32[896]{0:T(1024)S(1)} %copy-done.3, f32[896]{0:T(1024)S(1)} %copy-done.2, f32[192]{0:T(256)S(1)} %reshape.139, bf16[192,896]{1,0:T(8,128)(2,1)S(1)} %copy-done.15, ...), kind=kOutput, calls=%fused_computation.40 | convolution fusion | flops 310345728 | bytes 2990016 | tf_op jit(solution)/shard_map/dot_general | solution.py:60
  (115 shorter events, 39.2 us)
Async XLA Ops:
  0.0 6.0 %copy-start = (bf16[1,1,1,896,896]{4,3,2,1,0:T(8,128)(2,1)S(1)}, bf16[1,1,1,896,896]{4,3,2,1,0:T(8,128)(2,1)}, u32[]{:S(2)}) copy-start(bf16[1,1,1,896,896]{4,3,2,1,0:T(8,128)(2,1)} %param.13) | copy-start | bytes 4816900
  10.5 15.6 %collective-permute-start = (bf16[192,32,1]{0,2,1:T(2,128)(2,1)}, bf16[192,32,1]{0,2,1:T(2,128)(2,1)S(1)}, u32[]{:S(2)}, u32[]{:S(2)}) collective-permute-start(bf16[192,32,1]{0,2,1:T(2,128)(2,1)} %get-tuple-element.24), channel_id=1, source_target_pairs={{0,1},{1,2},{2,3},{3,4},{4,5},{5,6},{6,7},{8,9},{9,10},{10,11},{11... | collective-permute-start | bytes 36872 | tf_op jit(solution)/shard_map/ppermute | solution.py:22
  12.4 13.7 %collective-permute-start.3 = (bf16[192,32,1]{0,2,1:T(2,128)(2,1)}, bf16[192,32,1]{0,2,1:T(2,128)(2,1)}, u32[]{:S(2)}, u32[]{:S(2)}) collective-permute-start(bf16[192,32,1]{0,2,1:T(2,128)(2,1)} %get-tuple-element.25), channel_id=1, source_target_pairs={{1,0},{2,1},{3,2},{4,3},{5,4},{6,5},{7,6},{9,8},{10,9},{11,10},{12... | collective-permute-start | bytes 36872 | tf_op jit(solution)/shard_map/ppermute | solution.py:23
  16.6 8.4 %collective-permute-start.1 = (bf16[192,1,28]{0,2,1:T(8,128)(2,1)}, bf16[192,1,28]{0,2,1:T(8,128)(2,1)S(1)}, u32[]{:S(2)}, u32[]{:S(2)}) collective-permute-start(bf16[192,1,28]{0,2,1:T(8,128)(2,1)} %get-tuple-element.22), channel_id=1, source_target_pairs={{0,8},{8,16},{16,24},{24,32},{32,40},{40,48},{48,56},{1,9},{9,17},... | collective-permute-start | bytes 32264 | tf_op jit(solution)/shard_map/ppermute | solution.py:22
  20.1 5.9 %collective-permute-start.2 = (bf16[192,1,28]{0,2,1:T(8,128)(2,1)}, bf16[192,1,28]{0,2,1:T(8,128)(2,1)}, u32[]{:S(2)}, u32[]{:S(2)}) collective-permute-start(bf16[192,1,28]{0,2,1:T(8,128)(2,1)} %get-tuple-element.23), channel_id=1, source_target_pairs={{8,0},{16,8},{24,16},{32,24},{40,32},{48,40},{56,48},{9,1},{17,9},... | collective-permute-start | bytes 32264 | tf_op jit(solution)/shard_map/ppermute | solution.py:23
  29.6 6.3 %copy-start.11 = (s32[12]{0:T(128)S(1)}, s32[12]{0:T(128)}, u32[]{:S(2)}) copy-start(s32[12]{0:T(128)} %get-tuple-element.29) | copy-start | bytes 148
  29.6 6.4 %copy-start.4 = (s32[192]{0:T(256)S(1)}, s32[192]{0:T(256)}, u32[]{:S(2)}) copy-start(s32[192]{0:T(256)} %get-tuple-element.35) | copy-start | bytes 2308
  32.5 24.0 %collective-permute-start.4 = (bf16[192,896]{1,0:T(8,128)(2,1)}, bf16[192,896]{1,0:T(8,128)(2,1)}, u32[]{:S(2)}, u32[]{:S(2)}) collective-permute-start(bf16[192,896]{1,0:T(8,128)(2,1)} %fusion.52), channel_id=1, source_target_pairs={{0,64},{64,128},{128,192},{192,256},{256,320},{320,384},{384,448},... | collective-permute-start | bytes 1032200 | tf_op jit(solution)/shard_map/ppermute | solution.py:37
  37.1 19.4 %copy-start.1 = (bf16[192,896]{1,0:T(8,128)(2,1)}, bf16[192,896]{1,0:T(8,128)(2,1)S(1)}, u32[]{:S(2)}) copy-start(bf16[192,896]{1,0:T(8,128)(2,1)S(1)} %gather_fusion.2) | copy-start | bytes 1032196
  58.1 12.5 %copy-start.10 = (s32[12]{0:T(128)S(1)}, s32[12]{0:T(128)}, u32[]{:S(2)}) copy-start(s32[12]{0:T(128)} %get-tuple-element.27) | copy-start | bytes 148
  58.6 16.7 %collective-permute-start.5 = (bf16[192,32,1]{0,2,1:T(2,128)(2,1)S(1)}, bf16[192,32,1]{0,2,1:T(2,128)(2,1)S(1)}, u32[]{:S(2)}, u32[]{:S(2)}) collective-permute-start(bf16[192,32,1]{0,2,1:T(2,128)(2,1)S(1)} %get-tuple-element.20), channel_id=1, source_target_pairs={{0,1},{1,2},{2,3},{3,4},{4,5},{5,6},{6,7},{8,9},{9,10},{10,11},{11... | collective-permute-start | bytes 36872 | tf_op jit(solution)/shard_map/ppermute | solution.py:22
  60.5 14.8 %collective-permute-start.8 = (bf16[192,32,1]{0,2,1:T(2,128)(2,1)S(1)}, bf16[192,32,1]{0,2,1:T(2,128)(2,1)S(1)}, u32[]{:S(2)}, u32[]{:S(2)}) collective-permute-start(bf16[192,32,1]{0,2,1:T(2,128)(2,1)S(1)} %get-tuple-element.21), channel_id=1, source_target_pairs={{1,0},{2,1},{3,2},{4,3},{5,4},{6,5},{7,6},{9,8},{10,9},{11,10},{12... | collective-permute-start | bytes 36872 | tf_op jit(solution)/shard_map/ppermute | solution.py:23
  64.1 6.6 %collective-permute-start.6 = (bf16[192,1,28]{0,2,1:T(8,128)(2,1)S(1)}, bf16[192,1,28]{0,2,1:T(8,128)(2,1)S(1)}, u32[]{:S(2)}, u32[]{:S(2)}) collective-permute-start(bf16[192,1,28]{0,2,1:T(8,128)(2,1)S(1)} %get-tuple-element.18), channel_id=1, source_target_pairs={{0,8},{8,16},{16,24},{24,32},{32,40},{40,48},{48,56},{1,9},{9,17},... | collective-permute-start | bytes 32264 | tf_op jit(solution)/shard_map/ppermute | solution.py:22
  68.7 6.6 %collective-permute-start.7 = (bf16[192,1,28]{0,2,1:T(8,128)(2,1)S(1)}, bf16[192,1,28]{0,2,1:T(8,128)(2,1)S(1)}, u32[]{:S(2)}, u32[]{:S(2)}) collective-permute-start(bf16[192,1,28]{0,2,1:T(8,128)(2,1)S(1)} %get-tuple-element.19), channel_id=1, source_target_pairs={{8,0},{16,8},{24,16},{32,24},{40,32},{48,40},{56,48},{9,1},{17,9},... | collective-permute-start | bytes 32264 | tf_op jit(solution)/shard_map/ppermute | solution.py:23
  79.1 20.5 %collective-permute-start.9 = (bf16[192,896]{1,0:T(8,128)(2,1)}, bf16[192,896]{1,0:T(8,128)(2,1)S(1)}, u32[]{:S(2)}, u32[]{:S(2)}) collective-permute-start(bf16[192,896]{1,0:T(8,128)(2,1)} %fusion.55), channel_id=1, source_target_pairs={{0,64},{64,128},{128,192},{192,256},{256,320},{320,384},{384,448},... | collective-permute-start | bytes 1032200 | tf_op jit(solution)/shard_map/ppermute | solution.py:37
  101.4 14.9 %collective-permute-start.10 = (bf16[192,32,1]{0,2,1:T(2,128)(2,1)S(1)}, bf16[192,32,1]{0,2,1:T(2,128)(2,1)S(1)}, u32[]{:S(2)}, u32[]{:S(2)}) collective-permute-start(bf16[192,32,1]{0,2,1:T(2,128)(2,1)S(1)} %get-tuple-element.16), channel_id=1, source_target_pairs={{0,1},{1,2},{2,3},{3,4},{4,5},{5,6},{6,7},{8,9},{9,10},{10,11},{11... | collective-permute-start | bytes 36872 | tf_op jit(solution)/shard_map/ppermute | solution.py:22
  103.4 12.9 %collective-permute-start.13 = (bf16[192,32,1]{0,2,1:T(2,128)(2,1)S(1)}, bf16[192,32,1]{0,2,1:T(2,128)(2,1)S(1)}, u32[]{:S(2)}, u32[]{:S(2)}) collective-permute-start(bf16[192,32,1]{0,2,1:T(2,128)(2,1)S(1)} %get-tuple-element.17), channel_id=1, source_target_pairs={{1,0},{2,1},{3,2},{4,3},{5,4},{6,5},{7,6},{9,8},{10,9},{11,10},{12... | collective-permute-start | bytes 36872 | tf_op jit(solution)/shard_map/ppermute | solution.py:23
  107.0 5.9 %collective-permute-start.11 = (bf16[192,1,28]{0,2,1:T(8,128)(2,1)S(1)}, bf16[192,1,28]{0,2,1:T(8,128)(2,1)S(1)}, u32[]{:S(2)}, u32[]{:S(2)}) collective-permute-start(bf16[192,1,28]{0,2,1:T(8,128)(2,1)S(1)} %get-tuple-element.14), channel_id=1, source_target_pairs={{0,8},{8,16},{16,24},{24,32},{32,40},{40,48},{48,56},{1,9},{9,17},... | collective-permute-start | bytes 32264 | tf_op jit(solution)/shard_map/ppermute | solution.py:22
  110.7 5.6 %collective-permute-start.12 = (bf16[192,1,28]{0,2,1:T(8,128)(2,1)S(1)}, bf16[192,1,28]{0,2,1:T(8,128)(2,1)S(1)}, u32[]{:S(2)}, u32[]{:S(2)}) collective-permute-start(bf16[192,1,28]{0,2,1:T(8,128)(2,1)S(1)} %get-tuple-element.15), channel_id=1, source_target_pairs={{8,0},{16,8},{24,16},{32,24},{40,32},{48,40},{56,48},{9,1},{17,9},... | collective-permute-start | bytes 32264 | tf_op jit(solution)/shard_map/ppermute | solution.py:23
  119.3 18.9 %collective-permute-start.14 = (bf16[192,896]{1,0:T(8,128)(2,1)S(1)}, bf16[192,896]{1,0:T(8,128)(2,1)S(1)}, u32[]{:S(2)}, u32[]{:S(2)}) collective-permute-start(bf16[192,896]{1,0:T(8,128)(2,1)S(1)} %fusion.58), channel_id=1, source_target_pairs={{0,64},{64,128},{128,192},{192,256},{256,320},{320,384},{384,448},... | collective-permute-start | bytes 1032200 | tf_op jit(solution)/shard_map/ppermute | solution.py:37
  139.4 14.9 %collective-permute-start.15 = (bf16[192,32,1]{0,2,1:T(2,128)(2,1)S(1)}, bf16[192,32,1]{0,2,1:T(2,128)(2,1)S(1)}, u32[]{:S(2)}, u32[]{:S(2)}) collective-permute-start(bf16[192,32,1]{0,2,1:T(2,128)(2,1)S(1)} %get-tuple-element.12), channel_id=1, source_target_pairs={{0,1},{1,2},{2,3},{3,4},{4,5},{5,6},{6,7},{8,9},{9,10},{10,11},{11... | collective-permute-start | bytes 36872 | tf_op jit(solution)/shard_map/ppermute | solution.py:22
  141.3 13.0 %collective-permute-start.18 = (bf16[192,32,1]{0,2,1:T(2,128)(2,1)S(1)}, bf16[192,32,1]{0,2,1:T(2,128)(2,1)S(1)}, u32[]{:S(2)}, u32[]{:S(2)}) collective-permute-start(bf16[192,32,1]{0,2,1:T(2,128)(2,1)S(1)} %get-tuple-element.13), channel_id=1, source_target_pairs={{1,0},{2,1},{3,2},{4,3},{5,4},{6,5},{7,6},{9,8},{10,9},{11,10},{12... | collective-permute-start | bytes 36872 | tf_op jit(solution)/shard_map/ppermute | solution.py:23
  145.0 5.9 %collective-permute-start.16 = (bf16[192,1,28]{0,2,1:T(8,128)(2,1)S(1)}, bf16[192,1,28]{0,2,1:T(8,128)(2,1)S(1)}, u32[]{:S(2)}, u32[]{:S(2)}) collective-permute-start(bf16[192,1,28]{0,2,1:T(8,128)(2,1)S(1)} %get-tuple-element.10), channel_id=1, source_target_pairs={{0,8},{8,16},{16,24},{24,32},{32,40},{40,48},{48,56},{1,9},{9,17},... | collective-permute-start | bytes 32264 | tf_op jit(solution)/shard_map/ppermute | solution.py:22
  148.6 5.6 %collective-permute-start.17 = (bf16[192,1,28]{0,2,1:T(8,128)(2,1)S(1)}, bf16[192,1,28]{0,2,1:T(8,128)(2,1)S(1)}, u32[]{:S(2)}, u32[]{:S(2)}) collective-permute-start(bf16[192,1,28]{0,2,1:T(8,128)(2,1)S(1)} %get-tuple-element.11), channel_id=1, source_target_pairs={{8,0},{16,8},{24,16},{32,24},{40,32},{48,40},{56,48},{9,1},{17,9},... | collective-permute-start | bytes 32264 | tf_op jit(solution)/shard_map/ppermute | solution.py:23
  (14 other events, 35.6 us)
where the time goes:
time: 159 us; the launch traced here: 158 us
  waiting for transfers between devices  64.9 us (41%)
  starting transfers between devices  53.6 us (34%)
  local copies, waits for them, and re-layouts  16.3 us (10%)
  matrix products  15.2 us (10%)
  other arithmetic  7.73 us (5%)
    ppermute x3, waiting for transfers between devices, shifted(): return lax.ppermute(x, axis, pairs)  52.4 us
    ppermute x8, starting transfers between devices, with_halo(): lax.ppermute(first, axis, [(b, a) for a, b in up])  23.2 us
    ppermute x8, starting transfers between devices, with_halo(): lax.ppermute(last, axis, up)  23 us
    ppermute x8, waiting for transfers between devices, with_halo(): lax.ppermute(first, axis, [(b, a) for a, b in up])  12.4 us
    dot_general x4, matrix products, advance(): jnp.dot(coupled.reshape(slot_count, FX * FY), map_second, preferred_eleme...  10.8 us
    ppermute x3, starting transfers between devices, shifted(): return lax.ppermute(x, axis, pairs)  7.39 us
    dot_general x4, matrix products, advance(): jnp.dot(start_trace, map_first, preferred_element_type=jnp.float32)  4.43 us
    gather x4, local copies, waits for them, and re-layouts, local(): jnp.take(source[0, round_number, :, 0, 0, :], assignment[round_number], a...  4.16 us
  transfers between devices with their start and end apart: 19, of which 7 were waited for; matrix products, arithmetic and copies ran while one was open for 4% of the time, Pallas kernels for 0%

commit v1 on v0

v1 whole, which is shorter than its diff:
```python
import jax
import jax.numpy as jnp
from jax import lax
from jax.experimental import pallas as pl
from jax.experimental.pallas import tpu as pltpu
from jax.sharding import PartitionSpec as P

FX = 32
FY = 28
M = FX * FY
SHOT_BATCH = 16
SLOTS = 192
ROUNDS = 4

CHUNKS = 4
CH = SLOTS // CHUNKS
NB = CH // SHOT_BATCH
LANES = 128
coupling_weight = 0.25

MESH = pl.DeviceIdType.MESH
BF = jnp.bfloat16
F32 = jnp.float32

CROSS_FROM = 3
CROSS_TO = 4
CROSS_VIA = 0
RELAY = True


def cross_cut(c):
    return 512 if c % 2 == 0 else 384


def own_face_cell(k):
    return jnp.where(
        k < 32,
        jnp.where(k < FY, k, -1),
        jnp.where(
            k < 64,
            jnp.where(k < 32 + FY, M - FY + k - 32, -1),
            jnp.where(k < 96, (k - 64) * FY, (k - 96) * FY + FY - 1),
        ),
    )


def far_face_cell(k):
    return jnp.where(
        k < 32,
        jnp.where(k < FY, M - FY + k, -1),
        jnp.where(
            k < 64,
            jnp.where(k < 32 + FY, k - 32, -1),
            jnp.where(k < 96, (k - 64) * FY + FY - 1, (k - 96) * FY),
        ),
    )


def kernel(
    arrival_ref,
    source_ref,
    assign_ref,
    counts_ref,
    first_ref,
    second_ref,
    damping_ref,
    out_ref,
    inc_v,
    src_v,
    first_v,
    second_v,
    pick_v,
    face_sel_v,
    halo_sel_v,
    start_v,
    mapped_v,
    faces_v,
    halo_v,
    h_v,
    relay_v,
    load_sem,
    face_send,
    face_recv,
    down_send,
    down_recv,
    relay_send,
    relay_recv,
    relay_out,
    relay_in,
    out_sem,
):
    depth = lax.axis_index("depth")
    gx = lax.axis_index("gx")
    gy = lax.axis_index("gy")
    layers = lax.axis_size("depth")
    sides = []
    for axis, at in (("gx", gx), ("gy", gy)):
        size = lax.axis_size(axis)
        sides.append((axis, at - 1, at > 0))
        sides.append((axis, at + 1, at < size - 1))
    has_up = depth > 0
    has_down = depth < layers - 1

    barrier = pltpu.get_barrier_semaphore()
    partners = [(axis, to, there) for axis, to, there in sides]
    partners.append(("depth", depth - 1, has_up))
    partners.append(("depth", depth + 1, has_down))
    relaying = RELAY and layers > CROSS_TO
    if relaying:
        partners.append(("depth", CROSS_VIA, depth == CROSS_FROM))
        partners.append(("depth", CROSS_FROM, depth == CROSS_VIA))
        partners.append(("depth", CROSS_TO, depth == CROSS_VIA))
        partners.append(("depth", CROSS_VIA, depth == CROSS_TO))
    for axis, to, there in partners:

        @pl.when(there)
        def _():
            pl.semaphore_signal(barrier, inc=1, device_id={axis: to}, device_id_type=MESH)

    def load(src, dst, at):
        return pltpu.make_async_copy(src, dst, load_sem.at[at])

    loads = [
        load(source_ref.at[pl.ds(0, SLOTS)], src_v.at[pl.ds(0, SLOTS)], 0),
        load(arrival_ref, inc_v.at[pl.ds(0, SLOTS)], 1),
        load(first_ref, first_v, 2),
        load(second_ref, second_v, 3),
        load(source_ref.at[pl.ds(SLOTS, 3 * SLOTS)], src_v.at[pl.ds(SLOTS, 3 * SLOTS)], 4),
    ]
    for one in loads:
        one.start()

    sub = lax.broadcasted_iota(jnp.int32, (SLOTS, SLOTS), 0)
    lane = lax.broadcasted_iota(jnp.int32, (SLOTS, SLOTS), 1)
    for r in range(ROUNDS):
        row = jnp.broadcast_to(assign_ref[r : r + 1, :].astype(F32), (SLOTS, SLOTS))
        column = jnp.sum(jnp.where(sub == lane, row, 0.0), axis=1, keepdims=True)
        pick_v[r * SLOTS : (r + 1) * SLOTS, :] = (column == lane.astype(F32)).astype(F32).astype(BF)
    cells = lax.broadcasted_iota(jnp.int32, (M, LANES), 0)
    faces = own_face_cell(lax.broadcasted_iota(jnp.int32, (M, LANES), 1))
    face_sel_v[...] = (cells == faces).astype(F32).astype(BF)
    cells = lax.broadcasted_iota(jnp.int32, (LANES, M), 1)
    faces = far_face_cell(lax.broadcasted_iota(jnp.int32, (LANES, M), 0))
    halo_sel_v[...] = (cells == faces).astype(F32).astype(BF)

    for k, (_, _, there) in enumerate(sides):

        @pl.when(jnp.logical_not(there))
        def _():
            halo_v[k] = jnp.zeros((ROUNDS * SLOTS, LANES), BF)

    @pl.when(jnp.logical_not(has_up))
    def _():
        inc_v[pl.ds(SLOTS, 3 * SLOTS), :] = jnp.zeros((3 * SLOTS, M), BF)

    def rows_of(t):
        return pl.ds(pl.multiple_of(t * CH, SHOT_BATCH), CH)

    def active_of(r, c):
        unit = r - depth + layers - 1
        inside = lax.broadcasted_iota(jnp.int32, (CH, LANES), 0)
        limit = jnp.broadcast_to(counts_ref[unit, c * NB], (CH, LANES))
        for b in range(1, NB):
            limit = jnp.where(
                inside < b * SHOT_BATCH, limit, counts_ref[unit, c * NB + b] + b * SHOT_BATCH
            )
        return jnp.concatenate([inside < limit] * (M // LANES), axis=1)

    def face_copy(k, t):
        axis, to, _ = sides[k]
        return pltpu.make_async_remote_copy(
            src_ref=faces_v.at[rows_of(t)],
            dst_ref=halo_v.at[k ^ 1, rows_of(t)],
            send_sem=face_send.at[k, t],
            recv_sem=face_recv.at[k ^ 1, t],
            device_id={axis: to},
            device_id_type=MESH,
        )

    def face_arrival(k, t):
        axis, to, _ = sides[k]
        return pltpu.make_async_remote_copy(
            src_ref=faces_v.at[rows_of(t)],
            dst_ref=halo_v.at[k, rows_of(t)],
            send_sem=face_send.at[k, t],
            recv_sem=face_recv.at[k, t],
            device_id={axis: to},
            device_id_type=MESH,
        )

    def down_copy(t, lanes):
        return pltpu.make_async_remote_copy(
            src_ref=h_v.at[rows_of(t), lanes],
            dst_ref=inc_v.at[rows_of(t + CHUNKS), lanes],
            send_sem=down_send.at[t],
            recv_sem=down_recv.at[t],
            device_id={"depth": depth + 1},
            device_id_type=MESH,
        )

    def to_relay(t, lanes):
        return pltpu.make_async_remote_copy(
            src_ref=h_v.at[rows_of(t), lanes],
            dst_ref=relay_v.at[rows_of(t), lanes],
            send_sem=relay_send.at[t],
            recv_sem=relay_recv.at[t],
            device_id={"depth": CROSS_VIA},
            device_id_type=MESH,
        )

    def from_relay(t, lanes):
        return pltpu.make_async_remote_copy(
            src_ref=relay_v.at[rows_of(t), lanes],
            dst_ref=inc_v.at[rows_of(t + CHUNKS), lanes],
            send_sem=relay_out.at[t],
            recv_sem=relay_in.at[t],
            device_id={"depth": CROSS_TO},
            device_id_type=MESH,
        )

    whole = pl.ds(0, M)

    def straight(c):
        return pl.ds(0, cross_cut(c))

    def passed(c):
        return pl.ds(cross_cut(c), M - cross_cut(c))

    def map_faces(r, c):
        t = r * CHUNKS + c
        rows = rows_of(t)
        if relaying:

            @pl.when((r > 0) & has_up & (depth != CROSS_TO))
            def _():
                down_copy(t - CHUNKS, whole).wait_recv()

            @pl.when((r > 0) & (depth == CROSS_TO))
            def _():
                down_copy(t - CHUNKS, straight(c)).wait_recv()
                from_relay(t - CHUNKS, passed(c)).wait_recv()

        else:

            @pl.when((r > 0) & has_up)
            def _():
                down_copy(t - CHUNKS, whole).wait_recv()

        shots = src_v[pl.ds(pl.multiple_of(r * SLOTS, SHOT_BATCH), SLOTS), :]
        picked = jnp.dot(pick_v[rows, :], shots, preferred_element_type=F32)
        start = jnp.where(active_of(r, c), picked + inc_v[rows, :].astype(F32), 0.0).astype(BF)
        start_v[rows, :] = start
        mapped = jnp.dot(start, first_v[...], preferred_element_type=F32).astype(BF)
        mapped_v[rows, :] = mapped
        faces_v[rows, :] = jnp.dot(mapped, face_sel_v[...], preferred_element_type=F32).astype(BF)

    def send_faces(r, c):
        for k, (_, _, there) in enumerate(sides):

            @pl.when(there)
            def _():
                face_copy(k, r * CHUNKS + c).start()

    def couple(r, c):
        t = r * CHUNKS + c
        rows = rows_of(t)
        for k, (_, _, there) in enumerate(sides):

            @pl.when(there)
            def _():
                face_arrival(k, t).wait_recv()

        spot = lax.broadcasted_iota(jnp.int32, (CH, LANES), 1)
        low = jnp.where(spot < 32, halo_v[1, rows, :].astype(F32), halo_v[0, rows, :].astype(F32))
        high = jnp.where(spot < 96, halo_v[3, rows, :].astype(F32), halo_v[2, rows, :].astype(F32))
        halo = jnp.where(spot < 64, low, high).astype(BF)
        around = jnp.dot(halo, halo_sel_v[...], preferred_element_type=F32)
        mapped = mapped_v[rows, :].astype(F32)
        cell = lax.broadcasted_iota(jnp.int32, (CH, M), 1)
        across = lax.rem(cell, FY)
        around += jnp.where(cell < M - FY, pltpu.roll(mapped, M - FY, 1), 0.0)
        around += jnp.where(cell >= FY, pltpu.roll(mapped, FY, 1), 0.0)
        around += jnp.where(across < FY - 1, pltpu.roll(mapped, M - 1, 1), 0.0)
        around += jnp.where(across > 0, pltpu.roll(mapped, 1, 1), 0.0)
        coupled = (mapped + coupling_weight * around).astype(BF)
        image = jnp.dot(coupled, second_v[...], preferred_element_type=F32)
        damping = damping_ref[...]
        blended = damping * image + (1.0 - damping) * start_v[rows, :].astype(F32)
        h_v[rows, :] = jnp.where(active_of(r, c), blended, 0.0).astype(BF)

        if relaying:

            @pl.when((r < ROUNDS - 1) & has_down & (depth != CROSS_FROM))
            def _():
                down_copy(t, whole).start()

            @pl.when((r < ROUNDS - 1) & (depth == CROSS_FROM))
            def _():
                to_relay(t, passed(c)).start()
                down_copy(t, straight(c)).start()

            @pl.when((r > 0) & (depth == CROSS_VIA))
            def _():
                to_relay(t - CHUNKS, passed(c)).wait_recv()
                from_relay(t - CHUNKS, passed(c)).start()

        else:

            @pl.when((r < ROUNDS - 1) & has_down)
            def _():
                down_copy(t, whole).start()

        @pl.when(r == ROUNDS - 1)
        def _():
            out_copy(t, c).start()

    def out_copy(t, c):
        return pltpu.make_async_copy(
            h_v.at[rows_of(t)], out_ref.at[pl.ds(c * CH, CH)], out_sem.at[c]
        )

    for one in loads[:3]:
        one.wait()

    def one_round(r, first):
        for c in range(CHUNKS):
            map_faces(r, c)
            if first and c == 0:
                pl.semaphore_wait(barrier, sum(there.astype(jnp.int32) for _, _, there in partners))

            send_faces(r, c)
            if c >= 2:
                if first and c == 2:
                    loads[3].wait()
                couple(r, c - 2)
        couple(r, CHUNKS - 2)
        couple(r, CHUNKS - 1)

    one_round(jnp.int32(0), True)
    loads[4].wait()

    def later_round(r, carry):
        one_round(r, False)
        return carry

    lax.fori_loop(1, ROUNDS, later_round, 0)

    for c in range(CHUNKS):
        out_copy((ROUNDS - 1) * CHUNKS + c, c).wait()

    def drain_faces(t, carry):
        for k, (_, _, there) in enumerate(sides):

            @pl.when(there)
            def _():
                face_copy(k, t).wait_send()

        return carry

    lax.fori_loop(0, ROUNDS * CHUNKS, drain_faces, 0)

    def drain_down(r, carry):
        for c in range(CHUNKS):
            t = r * CHUNKS + c
            if relaying:

                @pl.when(has_down & (depth != CROSS_FROM))
                def _():
                    down_copy(t, whole).wait_send()

                @pl.when(depth == CROSS_FROM)
                def _():
                    down_copy(t, straight(c)).wait_send()
                    to_relay(t, passed(c)).wait_send()

                @pl.when(depth == CROSS_VIA)
                def _():
                    from_relay(t, passed(c)).wait_send()

            else:

                @pl.when(has_down)
                def _():
                    down_copy(t, whole).wait_send()

        return carry

    lax.fori_loop(0, ROUNDS - 1, drain_down, 0)


def local(arrival, source, assignment, counts, first_map, second_map, damping):
    steps = ROUNDS * CHUNKS
    slots = ROUNDS * SLOTS
    anywhere = pl.BlockSpec(memory_space=pl.ANY)
    vmem = pl.BlockSpec(memory_space=pltpu.VMEM)
    dma = pltpu.SemaphoreType.DMA
    units, batches = counts.shape[:2]
    result = pl.pallas_call(
        kernel,
        out_shape=jax.ShapeDtypeStruct((SLOTS, M), BF),
        in_specs=[
            anywhere,
            anywhere,
            vmem,
            pl.BlockSpec(memory_space=pltpu.SMEM),
            anywhere,
            anywhere,
            vmem,
        ],
        out_specs=anywhere,
        scratch_shapes=[
            pltpu.VMEM((slots, M), BF),
            pltpu.VMEM((slots, M), BF),
            pltpu.VMEM((M, M), BF),
            pltpu.VMEM((M, M), BF),
            pltpu.VMEM((slots, SLOTS), BF),
            pltpu.VMEM((M, LANES), BF),
            pltpu.VMEM((LANES, M), BF),
            pltpu.VMEM((slots, M), BF),
            pltpu.VMEM((slots, M), BF),
            pltpu.VMEM((slots, LANES), BF),
            pltpu.VMEM((4, slots, LANES), BF),
            pltpu.VMEM((slots, M), BF),
            pltpu.VMEM((slots, M), BF),
            dma((5,)),
            dma((4, steps)),
            dma((4, steps)),
            dma((steps,)),
            dma((steps,)),
            dma((steps,)),
            dma((steps,)),
            dma((steps,)),
            dma((steps,)),
            dma((CHUNKS,)),
        ],
        compiler_params=pltpu.CompilerParams(collective_id=0, has_side_effects=True),
        name="sweep",
    )(
        arrival.reshape(SLOTS, M),
        source.reshape(slots, M),
        assignment,
        counts.reshape(units, batches),
        first_map.reshape(M, M),
        second_map.reshape(M, M),
        damping.reshape(1, M),
    )
    return result.reshape(1, SLOTS, 1, 1, M)


def solution(mesh):
    return jax.shard_map(
        local,
        mesh=mesh,
        in_specs=(
            P("depth", None, "gx", "gy", None),
            P("depth", None, None, "gx", "gy", None),
            P(),
            P(None, None, "gx", "gy"),
            P("depth", "gx", "gy", None, None),
            P("depth", "gx", "gy", None, None),
            P("depth", "gx", "gy", None),
        ),
        out_specs=P("depth", None, "gx", "gy", None),
        check_vma=False,
    )
```

time: 159 us -> 59.9 us (0.38)
  the two profiles are of different devices: /device:TPU:328 before, /device:TPU:408 now
where the time goes in v1:
time: 59.9 us; the launch traced here: 59.7 us
  Pallas kernels  56.6 us (94%)
  local copies, waits for them, and re-layouts  3.02 us (5%)
    pallas_call x1, Pallas kernels, local(): pl.pallas_call(kernel, out_shape=jax.ShapeDtypeStruct((SLOTS, M), BF), in...  56.6 us
    unnamed x2, local copies, waits for them, and re-layouts  3.02 us

profile of v1, /device:TPU:408, one launch (start us, length us, event | category | flops | bytes accessed | tf_op | source)
XLA Modules:
  0.0 59.7 jit_solution(16400241400279321680)
XLA Ops:
  0.0 1.3 %copy.10 = s32[11,12,1,1]{1,0,2,3:T(8,128)} copy(s32[11,12,1,1]{1,3,2,0:T(1,128)} %param.10) | data formatting | bytes 1056
  1.3 56.6 %sweep.1 = bf16[192,896]{1,0:T(8,128)(2,1)} custom-call(bf16[192,896]{1,0:T(8,128)(2,1)} %bitcast.13, bf16[768,896]{1,0:T(8,128)(2,1)} %bitcast.11, s32[4,192]{1,0:T(4,128)} %assign_ref.1, s32[11,12]{1,0:T(8,128)} %bitcast.14, bf16[896,896]{1,0:T(8,128)(2,1)} %bitcast.9, bf16[896,896]{1,0:T(8,128)(2,1)} %bitcast.10, f32[1,896]{1,0:T(1,128)} %bitcast.15), custom_call_target="tpu_custom_call" | custom-call | tf_op jit(solution)/shard_map/sweep/pallas_call | solution.py:398
  57.9 1.7 %copy.12 = bf16[1,192,1,1,896]{4,1,3,2,0:T(8,128)(2,1)} copy(bf16[1,192,1,1,896]{4,1,3,2,0:T(8,128)(2,1)} %bitcast.12) | data formatting | bytes 688128

commit v2 on v1

--- a/solution.py
+++ b/solution.py
@@ -12,7 +12,7 @@
 SLOTS = 192
 ROUNDS = 4
 
-CHUNKS = 4
+CHUNKS = 3
 CH = SLOTS // CHUNKS
 NB = CH // SHOT_BATCH
 LANES = 128
@@ -24,12 +24,9 @@
 
 CROSS_FROM = 3
 CROSS_TO = 4
-CROSS_VIA = 0
+CROSS_VIA = (0, 2, 1)
+SHARE = CH // (1 + len(CROSS_VIA))
 RELAY = True
-
-
-def cross_cut(c):
-    return 512 if c % 2 == 0 else 384
 
 
 def own_face_cell(k):
@@ -72,8 +69,11 @@
     pick_v,
     face_sel_v,
     halo_sel_v,
-    start_v,
-    mapped_v,
+    first_faces_v,
+    halo_map_v,
+    weight_v,
+    damping_v,
+    base_v,
     faces_v,
     halo_v,
     h_v,
@@ -107,10 +107,11 @@
     partners.append(("depth", depth + 1, has_down))
     relaying = RELAY and layers > CROSS_TO
     if relaying:
-        partners.append(("depth", CROSS_VIA, depth == CROSS_FROM))
-        partners.append(("depth", CROSS_FROM, depth == CROSS_VIA))
-        partners.append(("depth", CROSS_TO, depth == CROSS_VIA))
-        partners.append(("depth", CROSS_VIA, depth == CROSS_TO))
+        for via in CROSS_VIA:
+            for end in (CROSS_FROM, CROSS_TO):
+                if abs(via - end) > 1:
+                    partners.append(("depth", via, depth == end))
+                    partners.append(("depth", end, depth == via))
     for axis, to, there in partners:
 
         @pl.when(there)
@@ -132,10 +133,14 @@
 
     sub = lax.broadcasted_iota(jnp.int32, (SLOTS, SLOTS), 0)
     lane = lax.broadcasted_iota(jnp.int32, (SLOTS, SLOTS), 1)
-    for r in range(ROUNDS):
+
+    def fill_pick(r):
         row = jnp.broadcast_to(assign_ref[r : r + 1, :].astype(F32), (SLOTS, SLOTS))
         column = jnp.sum(jnp.where(sub == lane, row, 0.0), axis=1, keepdims=True)
-        pick_v[r * SLOTS : (r + 1) * SLOTS, :] = (column == lane.astype(F32)).astype(F32).astype(BF)
+        hot = (column == lane.astype(F32)).astype(F32)
+        pick_v[r * SLOTS : (r + 1) * SLOTS, :] = hot.astype(BF)
+
+    fill_pick(0)
     cells = lax.broadcasted_iota(jnp.int32, (M, LANES), 0)
     faces = own_face_cell(lax.broadcasted_iota(jnp.int32, (M, LANES), 1))
     face_sel_v[...] = (cells == faces).astype(F32).astype(BF)
@@ -143,6 +148,16 @@
     faces = far_face_cell(lax.broadcasted_iota(jnp.int32, (LANES, M), 0))
     halo_sel_v[...] = (cells == faces).astype(F32).astype(BF)
 
+    cells = lax.broadcasted_iota(jnp.int32, (8, M), 1)
+    across = lax.rem(cells, FY)
+    for k, inside in enumerate((cells < M - FY, cells >= FY, across < FY - 1, across > 0)):
+        weight_v[k] = jnp.where(inside, coupling_weight, 0.0)
+    damping_v[0] = jnp.broadcast_to(damping_ref[...], (8, M))
+    damping_v[1] = 1.0 - damping_v[0]
+
+    def on_rows(eight):
+        return jnp.concatenate([eight] * (CH // 8), axis=0)
+
     for k, (_, _, there) in enumerate(sides):
 
         @pl.when(jnp.logical_not(there))
@@ -159,10 +174,10 @@
     def active_of(r, c):
         unit = r - depth + layers - 1
         inside = lax.broadcasted_iota(jnp.int32, (CH, LANES), 0)
-        limit = jnp.broadcast_to(counts_ref[unit, c * NB], (CH, LANES))
+        limit = jnp.broadcast_to(counts_ref[unit, 0, c * NB], (CH, LANES))
         for b in range(1, NB):
             limit = jnp.where(
-                inside < b * SHOT_BATCH, limit, counts_ref[unit, c * NB + b] + b * SHOT_BATCH
+                inside < b * SHOT_BATCH, limit, counts_ref[unit, 0, c * NB + b] + b * SHOT_BATCH
             )
         return jnp.concatenate([inside < limit] * (M // LANES), axis=1)
 
@@ -188,71 +203,99 @@
             device_id_type=MESH,
         )
 
-    def down_copy(t, lanes):
+    def share_of(t, part):
+        return pl.ds(pl.multiple_of(t * CH + part * SHARE, SHOT_BATCH), SHARE)
+
+    def down_copy(t, share=None):
+        here = rows_of(t) if share is None else share_of(t, share)
+        there = rows_of(t + CHUNKS) if share is None else share_of(t + CHUNKS, share)
         return pltpu.make_async_remote_copy(
-            src_ref=h_v.at[rows_of(t), lanes],
-            dst_ref=inc_v.at[rows_of(t + CHUNKS), lanes],
+            src_ref=h_v.at[here],
+            dst_ref=inc_v.at[there],
             send_sem=down_send.at[t],
             recv_sem=down_recv.at[t],
             device_id={"depth": depth + 1},
             device_id_type=MESH,
         )
 
-    def to_relay(t, lanes):
+    def relay_rows(t):
+        return pl.ds(pl.multiple_of(t * SHARE, SHOT_BATCH), SHARE)
+
+    def to_relay(t, q):
         return pltpu.make_async_remote_copy(
-            src_ref=h_v.at[rows_of(t), lanes],
-            dst_ref=relay_v.at[rows_of(t), lanes],
-            send_sem=relay_send.at[t],
+            src_ref=h_v.at[share_of(t, 1 + q)],
+            dst_ref=relay_v.at[relay_rows(t)],
+            send_sem=relay_send.at[q, t],
             recv_sem=relay_recv.at[t],
-            device_id={"depth": CROSS_VIA},
+            device_id={"depth": CROSS_VIA[q]},
             device_id_type=MESH,
         )
 
-    def from_relay(t, lanes):
+    def from_relay(t, q):
         return pltpu.make_async_remote_copy(
-            src_ref=relay_v.at[rows_of(t), lanes],
-            dst_ref=inc_v.at[rows_of(t + CHUNKS), lanes],
+            src_ref=relay_v.at[relay_rows(t)],
+            dst_ref=inc_v.at[share_of(t + CHUNKS, 1 + q)],
             send_sem=relay_out.at[t],
-            recv_sem=relay_in.at[t],
+            recv_sem=relay_in.at[q, t],
             device_id={"depth": CROSS_TO},
             device_id_type=MESH,
         )
 
-    whole = pl.ds(0, M)
-
-    def straight(c):
-        return pl.ds(0, cross_cut(c))
-
-    def passed(c):
-        return pl.ds(cross_cut(c), M - cross_cut(c))
-
-    def map_faces(r, c):
+    def pass_on(r, c):
+        if relaying:
+            t = r * CHUNKS + c
+            for q, via in enumerate(CROSS_VIA):
+
+                @pl.when((r < ROUNDS - 1) & (depth == via))
+                def _():
+                    to_relay(t, q).wait_recv()
+                    from_relay(t, q).start()
+
+    def advance(r, c, first):
         t = r * CHUNKS + c
         rows = rows_of(t)
-        if relaying:
-
-            @pl.when((r > 0) & has_up & (depth != CROSS_TO))
-            def _():
-                down_copy(t - CHUNKS, whole).wait_recv()
-
-            @pl.when((r > 0) & (depth == CROSS_TO))
-            def _():
-                down_copy(t - CHUNKS, straight(c)).wait_recv()
-                from_relay(t - CHUNKS, passed(c)).wait_recv()
-
-        else:
-
-            @pl.when((r > 0) & has_up)
-            def _():
-                down_copy(t - CHUNKS, whole).wait_recv()
-
         shots = src_v[pl.ds(pl.multiple_of(r * SLOTS, SHOT_BATCH), SLOTS), :]
         picked = jnp.dot(pick_v[rows, :], shots, preferred_element_type=F32)
+        if relaying:
+
+            @pl.when((r > 0) & has_up & (depth != CROSS_TO))
+            def _():
+                down_copy(t - CHUNKS).wait_recv()
+
+            @pl.when((r > 0) & (depth == CROSS_TO))
+            def _():
+                down_copy(t - CHUNKS, 0).wait_recv()
+                for q in range(len(CROSS_VIA)):
+                    from_relay(t - CHUNKS, q).wait_recv()
+
+        else:
+
+            @pl.when((r > 0) & has_up)
+            def _():
+                down_copy(t - CHUNKS).wait_recv()
+
         start = jnp.where(active_of(r, c), picked + inc_v[rows, :].astype(F32), 0.0).astype(BF)
-        start_v[rows, :] = start
-        mapped = jnp.dot(start, first_v[...], preferred_element_type=F32).astype(BF)
-        mapped_v[rows, :] = mapped
-        faces_v[rows, :] = jnp.dot(mapped, face_sel_v[...], preferred_element_type=F32).astype(BF)
+        if first:
+            mapped = jnp.dot(start, first_v[...], preferred_element_type=F32).astype(BF)
+            faces_v[rows, :] = jnp.dot(mapped, face_sel_v[...], preferred_element_type=F32).astype(BF)
+            if c == 0:
+                peers = sum(there.astype(jnp.int32) for _, _, there in partners)
+                pl.semaphore_wait(barrier, peers)
+            send_faces(r, c)
+            if c == 0:
+                loads[3].wait()
+        else:
+            faces = jnp.dot(start, first_faces_v[...], preferred_element_type=F32)
+            faces_v[rows, :] = faces.astype(BF)
+            send_faces(r, c)
+            mapped = jnp.dot(start, first_v[...], preferred_element_type=F32).astype(BF)
+        mapped = mapped.astype(F32)
+        coupled = mapped
+        for k, by in enumerate((M - FY, FY, M - 1, 1)):
+            coupled += on_rows(weight_v[k]) * pltpu.roll(mapped, by, 1)
+        image = jnp.dot(coupled.astype(BF), second_v[...], preferred_element_type=F32)
+        base = on_rows(damping_v[0]) * image + on_rows(damping_v[1]) * start.astype(F32)
+        base_v[c * CH : (c + 1) * CH, :] = base
 
     def send_faces(r, c):
         for k, (_, _, there) in enumerate(sides):
@@ -261,7 +304,7 @@
             def _():
                 face_copy(k, r * CHUNKS + c).start()
 
-    def couple(r, c):
+    def finish(r, c):
         t = r * CHUNKS + c
         rows = rows_of(t)
         for k, (_, _, there) in enumerate(sides):
@@ -274,41 +317,27 @@
         low = jnp.where(spot < 32, halo_v[1, rows, :].astype(F32), halo_v[0, rows, :].astype(F32))
         high = jnp.where(spot < 96, halo_v[3, rows, :].astype(F32), halo_v[2, rows, :].astype(F32))
         halo = jnp.where(spot < 64, low, high).astype(BF)
-        around = jnp.dot(halo, halo_sel_v[...], preferred_element_type=F32)
-        mapped = mapped_v[rows, :].astype(F32)
-        cell = lax.broadcasted_iota(jnp.int32, (CH, M), 1)
-        across = lax.rem(cell, FY)
-        around += jnp.where(cell < M - FY, pltpu.roll(mapped, M - FY, 1), 0.0)
-        around += jnp.where(cell >= FY, pltpu.roll(mapped, FY, 1), 0.0)
-        around += jnp.where(across < FY - 1, pltpu.roll(mapped, M - 1, 1), 0.0)
-        around += jnp.where(across > 0, pltpu.roll(mapped, 1, 1), 0.0)
-        coupled = (mapped + coupling_weight * around).astype(BF)
-        image = jnp.dot(coupled, second_v[...], preferred_element_type=F32)
-        damping = damping_ref[...]
-        blended = damping * image + (1.0 - damping) * start_v[rows, :].astype(F32)
+        added = jnp.dot(halo, halo_map_v[...], preferred_element_type=F32)
+        blended = base_v[c * CH : (c + 1) * CH, :] + on_rows(damping_v[0]) * added
         h_v[rows, :] = jnp.where(active_of(r, c), blended, 0.0).astype(BF)
 
         if relaying:
 
             @pl.when((r < ROUNDS - 1) & has_down & (depth != CROSS_FROM))
             def _():
-                down_copy(t, whole).start()
+                down_copy(t).start()
 
             @pl.when((r < ROUNDS - 1) & (depth == CROSS_FROM))
             def _():
-                to_relay(t, passed(c)).start()
-                down_copy(t, straight(c)).start()
-
-            @pl.when((r > 0) & (depth == CROSS_VIA))
-            def _():
-                to_relay(t - CHUNKS, passed(c)).wait_recv()
-                from_relay(t - CHUNKS, passed(c)).start()
+                for q in range(len(CROSS_VIA)):
+                    to_relay(t, q).start()
+                down_copy(t, 0).start()
 
         else:
 
             @pl.when((r < ROUNDS - 1) & has_down)
             def _():
-                down_copy(t, whole).start()
+                down_copy(t).start()
 
         @pl.when(r == ROUNDS - 1)
         def _():
@@ -323,20 +352,26 @@
         one.wait()
 
     def one_round(r, first):
+        lag = 2 if first else 1
         for c in range(CHUNKS):
-            map_faces(r, c)
-            if first and c == 0:
-                pl.semaphore_wait(barrier, sum(there.astype(jnp.int32) for _, _, there in partners))
-
-            send_faces(r, c)
-            if c >= 2:
-                if first and c == 2:
-                    loads[3].wait()
-                couple(r, c - 2)
-        couple(r, CHUNKS - 2)
-        couple(r, CHUNKS - 1)
+            advance(r, c, first)
+            if c < CHUNKS - 1 and not first:
+                pass_on(r - 1, c + 1)
+            if c == lag and first:
+                rows = jnp.dot(halo_sel_v[...], second_v[...], preferred_element_type=F32)
+                halo_map_v[...] = (coupling_weight * rows).astype(BF)
+            if c >= lag:
+                finish(r, c - lag)
+        for c in range(CHUNKS - lag, CHUNKS):
+            if c == CHUNKS - 1:
+                pass_on(r, 0)
+            finish(r, c)
 
     one_round(jnp.int32(0), True)
+    for r in range(1, ROUNDS):
+        fill_pick(r)
+    columns = jnp.dot(first_v[...], face_sel_v[...], preferred_element_type=F32)
+    first_faces_v[...] = columns.astype(BF)
     loads[4].wait()
 
     def later_round(r, carry):
@@ -366,22 +401,25 @@
 
                 @pl.when(has_down & (depth != CROSS_FROM))
                 def _():
-                    down_copy(t, whole).wait_send()
+                    down_copy(t).wait_send()
 
                 @pl.when(depth == CROSS_FROM)
                 def _():
-                    down_copy(t, straight(c)).wait_send()
-                    to_relay(t, passed(c)).wait_send()
-
-                @pl.when(depth == CROSS_VIA)
-                def _():
-                    from_relay(t, passed(c)).wait_send()
+                    down_copy(t, 0).wait_send()
+                    for q in range(len(CROSS_VIA)):
+                        to_relay(t, q).wait_send()
+
+                for q, via in enumerate(CROSS_VIA):
+
+                    @pl.when(depth == via)
+                    def _():
+                        from_relay(t, q).wait_send()
 
             else:
 
                 @pl.when(has_down)
                 def _():
-                    down_copy(t, whole).wait_send()
+                    down_copy(t).wait_send()
 
         return carry
 
@@ -397,7 +435,7 @@
     units, batches = counts.shape[:2]
     result = pl.pallas_call(
         kernel,
-        out_shape=jax.ShapeDtypeStruct((SLOTS, M), BF),
+        out_shape=pltpu.VMEM((SLOTS, M), BF),
         in_specs=[
             anywhere,
             anywhere,
@@ -416,30 +454,35 @@
             pltpu.VMEM((slots, SLOTS), BF),
             pltpu.VMEM((M, LANES), BF),
             pltpu.VMEM((LANES, M), BF),
-            pltpu.VMEM((slots, M), BF),
-            pltpu.VMEM((slots, M), BF),
+            pltpu.VMEM((M, LANES), BF),
+            pltpu.VMEM((LANES, M), BF),
+            pltpu.VMEM((4, 8, M), F32),
+            pltpu.VMEM((2, 8, M), F32),
+            pltpu.VMEM((SLOTS, M), F32),
             pltpu.VMEM((slots, LANES), BF),
             pltpu.VMEM((4, slots, LANES), BF),
             pltpu.VMEM((slots, M), BF),
-            pltpu.VMEM((slots, M), BF),
+            pltpu.VMEM((steps * SHARE, M), BF),
             dma((5,)),
             dma((4, steps)),
             dma((4, steps)),
             dma((steps,)),
             dma((steps,)),
+            dma((len(CROSS_VIA), steps)),
             dma((steps,)),
             dma((steps,)),
-            dma((steps,)),
-            dma((steps,)),
+            dma((len(CROSS_VIA), steps)),
             dma((CHUNKS,)),
         ],
-        compiler_params=pltpu.CompilerParams(collective_id=0, has_side_effects=True),
+        compiler_params=pltpu.CompilerParams(
+            collective_id=0, has_side_effects=True, vmem_limit_bytes=60_000_000
+        ),
         name="sweep",
     )(
         arrival.reshape(SLOTS, M),
         source.reshape(slots, M),
         assignment,
-        counts.reshape(units, batches),
+        counts.reshape(units, 1, batches),
         first_map.reshape(M, M),
         second_map.reshape(M, M),
         damping.reshape(1, M),

time: 59.9 us -> 49.5 us (0.83)
  the two profiles are of different devices: /device:TPU:408 before, /device:TPU:402 now
where the time goes in v2:
time: 49.5 us; the launch traced here: 49.4 us
  Pallas kernels  48.6 us (98%)
  local copies, waits for them, and re-layouts  0.73 us (1%)
    pallas_call x1, Pallas kernels, local(): pl.pallas_call(kernel, out_shape=pltpu.VMEM((SLOTS, M), BF), in_specs=[an...  48.6 us

profile of v2, /device:TPU:402, one launch (start us, length us, event | category | flops | bytes accessed | tf_op | source)
XLA Modules:
  0.0 49.4 jit_solution(460247132085575910)
XLA Ops:
  0.0 48.6 %sweep.1 = bf16[192,896]{1,0:T(8,128)(2,1)S(1)} custom-call(bf16[192,896]{1,0:T(8,128)(2,1)} %bitcast.11, bf16[768,896]{1,0:T(8,128)(2,1)} %bitcast.10, s32[4,192]{1,0:T(4,128)} %assign_ref.1, s32[11,1,12]{2,1,0:T(1,128)} %bitcast.12, bf16[896,896]{1,0:T(8,128)(2,1)} %bitcast.8, bf16[896,896]{1,0:T(8,128)(2,1)} %bitcast.9, f32[1,896]{1,0:T(1,128)} %bitcast.13), custom_call_target="tpu_custom_call" | custom-call | tf_op jit(solution)/shard_map/sweep/pallas_call | solution.py:436
  48.6 0.7 %copy.9 = bf16[1,192,1,1,896]{4,1,3,2,0:T(8,128)(2,1)} copy(bf16[1,192,1,1,896]{4,1,3,2,0:T(8,128)(2,1)S(1)} %bitcast.7) | data formatting | bytes 688128

commit v3 on v2

--- a/solution.py
+++ b/solution.py
@@ -24,8 +24,9 @@
 
 CROSS_FROM = 3
 CROSS_TO = 4
-CROSS_VIA = (0, 2, 1)
-SHARE = CH // (1 + len(CROSS_VIA))
+CROSS_VIA = (0, 1)
+SHARE = 16
+DIRECT = CH - SHARE * len(CROSS_VIA)
 RELAY = True
 
 
@@ -204,7 +205,10 @@
         )
 
     def share_of(t, part):
-        return pl.ds(pl.multiple_of(t * CH + part * SHARE, SHOT_BATCH), SHARE)
+        if part == 0:
+            return pl.ds(pl.multiple_of(t * CH, SHOT_BATCH), DIRECT)
+        first_row = t * CH + DIRECT + (part - 1) * SHARE
+        return pl.ds(pl.multiple_of(first_row, SHOT_BATCH), SHARE)
 
     def down_copy(t, share=None):
         here = rows_of(t) if share is None else share_of(t, share)
@@ -288,6 +292,18 @@
             faces = jnp.dot(start, first_faces_v[...], preferred_element_type=F32)
             faces_v[rows, :] = faces.astype(BF)
             send_faces(r, c)
+            if relaying and c == 0:
+
+                @pl.when(depth == CROSS_FROM)
+                def _():
+                    down_copy(t - 1, 0).start()
+
+            if relaying and c == 2:
+
+                @pl.when((r < ROUNDS - 1) & (depth == CROSS_FROM))
+                def _():
+                    down_copy(t - 2, 0).start()
+
             mapped = jnp.dot(start, first_v[...], preferred_element_type=F32).astype(BF)
         mapped = mapped.astype(F32)
         coupled = mapped
@@ -304,7 +320,7 @@
             def _():
                 face_copy(k, r * CHUNKS + c).start()
 
-    def finish(r, c):
+    def finish(r, c, first):
         t = r * CHUNKS + c
         rows = rows_of(t)
         for k, (_, _, there) in enumerate(sides):
@@ -331,7 +347,8 @@
             def _():
                 for q in range(len(CROSS_VIA)):
                     to_relay(t, q).start()
-                down_copy(t, 0).start()
+                if first and c < CHUNKS - 1 or 0 < c < CHUNKS - 1:
+                    down_copy(t, 0).start()
 
         else:
 
@@ -361,11 +378,11 @@
                 rows = jnp.dot(halo_sel_v[...], second_v[...], preferred_element_type=F32)
                 halo_map_v[...] = (coupling_weight * rows).astype(BF)
             if c >= lag:
-                finish(r, c - lag)
+                finish(r, c - lag, first)
         for c in range(CHUNKS - lag, CHUNKS):
             if c == CHUNKS - 1:
                 pass_on(r, 0)
-            finish(r, c)
+            finish(r, c, first)
 
     one_round(jnp.int32(0), True)
     for r in range(1, ROUNDS):
@@ -374,25 +391,22 @@
     first_faces_v[...] = columns.astype(BF)
     loads[4].wait()
 
+    def drain_faces(t, carry):
+        for k, (_, _, there) in enumerate(sides):
+
+            @pl.when(there)
+            def _():
+                face_copy(k, t).wait_send()
+
+        return carry
+
     def later_round(r, carry):
+        lax.fori_loop((r - 1) * CHUNKS, r * CHUNKS, drain_faces, 0)
         one_round(r, False)
         return carry
 
     lax.fori_loop(1, ROUNDS, later_round, 0)
-
-    for c in range(CHUNKS):
-        out_copy((ROUNDS - 1) * CHUNKS + c, c).wait()
-
-    def drain_faces(t, carry):
-        for k, (_, _, there) in enumerate(sides):
-
-            @pl.when(there)
-            def _():
-                face_copy(k, t).wait_send()
-
-        return carry
-
-    lax.fori_loop(0, ROUNDS * CHUNKS, drain_faces, 0)
+    lax.fori_loop((ROUNDS - 1) * CHUNKS, ROUNDS * CHUNKS, drain_faces, 0)
 
     def drain_down(r, carry):
         for c in range(CHUNKS):
@@ -424,6 +438,9 @@
         return carry
 
     lax.fori_loop(0, ROUNDS - 1, drain_down, 0)
+
+    for c in range(CHUNKS):
+        out_copy((ROUNDS - 1) * CHUNKS + c, c).wait()
 
 
 def local(arrival, source, assignment, counts, first_map, second_map, damping):

time: 49.5 us -> 48.7 us (0.984)
  the two profiles are of different devices: /device:TPU:402 before, /device:TPU:28 now
where the time goes in v3:
time: 48.7 us; the launch traced here: 48.6 us
  Pallas kernels  47.8 us (98%)
  local copies, waits for them, and re-layouts  0.73 us (1%)
    pallas_call x1, Pallas kernels, local(): pl.pallas_call(kernel, out_shape=pltpu.VMEM((SLOTS, M), BF), in_specs=[an...  47.8 us

profile of v3, /device:TPU:28, one launch (start us, length us, event | category | flops | bytes accessed | tf_op | source)
XLA Modules:
  0.0 48.6 jit_solution(5356365790797879697)
XLA Ops:
  0.0 47.8 %sweep.1 = bf16[192,896]{1,0:T(8,128)(2,1)S(1)} custom-call(bf16[192,896]{1,0:T(8,128)(2,1)} %bitcast.11, bf16[768,896]{1,0:T(8,128)(2,1)} %bitcast.10, s32[4,192]{1,0:T(4,128)} %assign_ref.1, s32[11,1,12]{2,1,0:T(1,128)} %bitcast.12, bf16[896,896]{1,0:T(8,128)(2,1)} %bitcast.8, bf16[896,896]{1,0:T(8,128)(2,1)} %bitcast.9, f32[1,896]{1,0:T(1,128)} %bitcast.13), custom_call_target="tpu_custom_call" | custom-call | tf_op jit(solution)/shard_map/sweep/pallas_call | solution.py:453
  47.8 0.7 %copy.9 = bf16[1,192,1,1,896]{4,1,3,2,0:T(8,128)(2,1)} copy(bf16[1,192,1,1,896]{4,1,3,2,0:T(8,128)(2,1)S(1)} %bitcast.7) | data formatting | bytes 688128
